TPU v7x, 32 devices: a whole 2x2x4 slice. The times are simulated.
32 devices in a mesh: ctx: 8 (over y, x, core), chan: 4 (over z).
Axes of the slice: x: 2, y: 2, z: 4, core: 2. Of those that a mesh axis runs over, the one named last changes fastest.
Arguments:
- signal: float32 [2048, 2048], P('chan', 'ctx'), may hold values from -6 to 6
- gate_in: float32 [2048, 2048], P('chan', 'ctx'), may hold values from -6 to 6
- filter_raw: float32 [2048, 2048], P('chan', 'ctx'), may hold values from -6 to 6
- short_kernel: float32 [2048, 7], P('chan'), may hold values from -2 to 2
- skip_gain: float32 [2048], P('chan'), may hold values from -4 to 4
- out_weight: float32 [2048, 2048], P(None, 'chan'), may hold values from -0.125 to 0.125
- cotangent: float32 [2048, 2048], P('chan', 'ctx'), may hold values from -6 to 6
Outputs:
- grad_gate: float32 [2048, 2048], P('chan', 'ctx')
- grad_signal: float32 [2048, 2048], P('chan', 'ctx')
- grad_filter: float32 [2048, 2048], P('chan', 'ctx')
- grad_kernel: float32 [2048, 7], P('chan')
- grad_skip: float32 [2048], P('chan')
All inputs are finite; a program needn't handle non-finite values.
Results may differ from a plain program's by a relative error of at most 0.00011.
Values sent between devices are 32-bit elements; how exact they have to be, the bound alone decides.
A program may use at most 128 MiB of HBM per device.

v0:
```python
import math
import jax
import jax.numpy as jnp
from jax import lax
from jax.sharding import PartitionSpec as P

HIGH = lax.Precision.HIGHEST


def passed_along(block, axis, distance):
    devices = range(lax.axis_size(axis))
    route = [(i - distance, i) for i in devices if i - distance in devices]
    return lax.ppermute(block, axis, route)


def angle_table(rows_len, cols_len, modulus):
    products = (
        jnp.arange(rows_len, dtype=jnp.int32)[:, None]
        * jnp.arange(cols_len, dtype=jnp.int32)[None, :]
        % modulus
    )
    return 2.0 * math.pi / modulus * products.astype(jnp.float32)


def rotate(real_part, imag_part, angles, sign):
    cosine = jnp.cos(angles)
    sine = sign * jnp.sin(angles)
    return (real_part * cosine - imag_part * sine, real_part * sine + imag_part * cosine)


def mix_last(real_part, imag_part, sign):
    span_len = real_part.shape[-1]
    angles = angle_table(span_len, span_len, span_len)
    cosine = jnp.cos(angles)
    sine = sign * jnp.sin(angles)

    def product_with(operand, table):
        return jnp.einsum("...a,ab->...b", operand, table, precision=HIGH)

    return (
        product_with(real_part, cosine) - product_with(imag_part, sine),
        product_with(real_part, sine) + product_with(imag_part, cosine),
    )


def mix_middle(real_part, imag_part, sign):
    span_len = real_part.shape[-2]
    angles = angle_table(span_len, span_len, span_len)
    cosine = jnp.cos(angles)
    sine = sign * jnp.sin(angles)

    def product_with(operand, table):
        return jnp.einsum("...ac,ab->...bc", operand, table, precision=HIGH)

    return (
        product_with(real_part, cosine) - product_with(imag_part, sine),
        product_with(real_part, sine) + product_with(imag_part, cosine),
    )


def split_len(length):
    inner_len = 128
    return (length // inner_len, inner_len)


def local_forward(real_part, imag_part):
    leading = real_part.shape[:-1]
    length = real_part.shape[-1]
    outer_len, inner_len = split_len(length)
    real_part = real_part.reshape(leading + (outer_len, inner_len))
    imag_part = imag_part.reshape(leading + (outer_len, inner_len))
    real_part, imag_part = mix_middle(real_part, imag_part, -1.0)
    real_part, imag_part = rotate(
        real_part, imag_part, angle_table(outer_len, inner_len, length), -1.0
    )
    real_part, imag_part = mix_last(real_part, imag_part, -1.0)
    return (real_part.reshape(leading + (length,)), imag_part.reshape(leading + (length,)))


def local_inverse(real_part, imag_part):
    leading = real_part.shape[:-1]
    length = real_part.shape[-1]
    outer_len, inner_len = split_len(length)
    real_part = real_part.reshape(leading + (outer_len, inner_len))
    imag_part = imag_part.reshape(leading + (outer_len, inner_len))
    real_part, imag_part = mix_last(real_part, imag_part, 1.0)
    real_part, imag_part = rotate(
        real_part, imag_part, angle_table(outer_len, inner_len, length), 1.0
    )
    real_part, imag_part = mix_middle(real_part, imag_part, 1.0)
    return (real_part.reshape(leading + (length,)), imag_part.reshape(leading + (length,)))


def block_twiddle(freqs, slice_len, modulus):
    offsets = lax.axis_index("ctx") * slice_len + jnp.arange(slice_len, dtype=jnp.int32)
    products = jnp.arange(freqs, dtype=jnp.int32)[:, None] * offsets[None, :] % modulus
    return 2.0 * math.pi / modulus * products.astype(jnp.float32)


def spectra(stacked):
    n_arrays, channels, length = stacked.shape
    devices = lax.axis_size("ctx")
    slice_len = length // devices
    freqs = 2 * devices
    modulus = freqs * length
    pieces = jnp.transpose(stacked.reshape(n_arrays, channels, devices, slice_len), (0, 2, 3, 1))
    arrived = lax.all_to_all(pieces, "ctx", split_axis=1, concat_axis=1, tiled=True)
    angles = angle_table(freqs, devices, freqs)
    real_part = jnp.einsum("qp,kprc->kqrc", jnp.cos(angles), arrived, precision=HIGH)
    imag_part = -jnp.einsum("qp,kprc->kqrc", jnp.sin(angles), arrived, precision=HIGH)
    twiddle = block_twiddle(freqs, slice_len, modulus)[:, :, None]
    real_part, imag_part = rotate(real_part, imag_part, twiddle, -1.0)
    arrived = lax.all_to_all(
        jnp.stack((real_part, imag_part)), "ctx", split_axis=2, concat_axis=3, tiled=True
    )
    arrived = jnp.moveaxis(arrived, 4, 2)
    return local_forward(arrived[0], arrived[1])


def signals(real_part, imag_part):
    real_part, imag_part = local_inverse(real_part, imag_part)
    n_arrays, channels, local_freqs, length = real_part.shape
    devices = lax.axis_size("ctx")
    slice_len = length // devices
    freqs = 2 * devices
    modulus = freqs * length
    stacked = jnp.moveaxis(jnp.stack((real_part, imag_part)), 2, 4)
    arrived = lax.all_to_all(stacked, "ctx", split_axis=3, concat_axis=2, tiled=True)
    twiddle = block_twiddle(freqs, slice_len, modulus)[:, :, None]
    real_part, imag_part = rotate(arrived[0], arrived[1], twiddle, 1.0)
    angles = angle_table(devices, freqs, freqs)
    samples = jnp.einsum("pq,kqrc->kprc", jnp.cos(angles), real_part, precision=HIGH) - jnp.einsum(
        "pq,kqrc->kprc", jnp.sin(angles), imag_part, precision=HIGH
    )
    arrived = lax.all_to_all(samples, "ctx", split_axis=1, concat_axis=2, tiled=True)
    return jnp.transpose(arrived.reshape(n_arrays, length, channels), (0, 2, 1)) / modulus


def spec_product(first, second, conjugate):
    first_real, first_imag = first
    if conjugate:
        first_imag = -first_imag
    second_real, second_imag = second
    return (
        first_real * second_real - first_imag * second_imag,
        first_real * second_imag + first_imag * second_real,
    )


def per_device(signal, gate_in, filter_raw, short_kernel, skip_gain, out_weight, cotangent):
    channels, length = signal.shape
    kernel_taps = short_kernel.shape[1]
    scale_factor = 1.0 / math.sqrt(length * lax.axis_size("ctx"))
    left_rim = passed_along(signal[:, length - (kernel_taps - 1) :], "ctx", 1)
    padded = jnp.concatenate((left_rim, signal), axis=1)
    conv_in = jnp.zeros_like(signal)
    for j in range(kernel_taps):
        conv_in = (
            conv_in
            + short_kernel[:, j : j + 1]
            * padded[:, kernel_taps - 1 - j : kernel_taps - 1 - j + length]
        )
    long_filter = filter_raw * scale_factor
    spec_real, spec_imag = spectra(jnp.stack((long_filter, conv_in)))
    filter_spec = (spec_real[0], spec_imag[0])
    value_spec = (spec_real[1], spec_imag[1])
    conv_real, conv_imag = spec_product(filter_spec, value_spec, False)
    long_conv = signals(conv_real[None], conv_imag[None])[0]
    grad_mix = jnp.dot(
        out_weight.T,
        lax.all_gather(cotangent, "chan", axis=0, tiled=True),
        precision=HIGH,
        preferred_element_type=jnp.float32,
    )
    grad_resp = grad_mix * gate_in
    grad_real, grad_imag = spectra(grad_resp[None])
    grad_spec = (grad_real[0], grad_imag[0])
    corr_spec = spec_product(filter_spec, grad_spec, True)
    filt_grad_spec = spec_product(value_spec, grad_spec, True)
    outputs = signals(
        jnp.stack((corr_spec[0], filt_grad_spec[0])), jnp.stack((corr_spec[1], filt_grad_spec[1]))
    )
    corr_part = outputs[0]
    filter_part = outputs[1]
    response = long_conv + skip_gain[:, None] * conv_in
    grad_gate = grad_mix * response
    grad_value = corr_part + skip_gain[:, None] * grad_resp
    grad_filter = filter_part * scale_factor
    right_rim = passed_along(grad_value[:, : kernel_taps - 1], "ctx", -1)
    extended = jnp.concatenate((grad_value, right_rim), axis=1)
    grad_signal = jnp.zeros_like(grad_value)
    for j in range(kernel_taps):
        grad_signal = grad_signal + short_kernel[:, j : j + 1] * extended[:, j : j + length]
    kernel_part = jnp.stack(
        [
            jnp.sum(
                grad_value * padded[:, kernel_taps - 1 - j : kernel_taps - 1 - j + length], axis=1
            )
            for j in range(kernel_taps)
        ],
        axis=1,
    )
    skip_part = jnp.sum(grad_resp * conv_in, axis=1)
    skip_sum, kernel_sum = lax.psum((skip_part, kernel_part), "ctx")
    return (grad_gate, grad_signal, grad_filter, kernel_sum * scale_factor, skip_sum * scale_factor)


def solution(mesh):
    placed = (
        P("chan", "ctx"),
        P("chan", "ctx"),
        P("chan", "ctx"),
        P("chan", None),
        P("chan"),
        P(None, "chan"),
        P("chan", "ctx"),
    )
    return jax.shard_map(
        per_device,
        mesh=mesh,
        in_specs=placed,
        out_specs=(
            P("chan", "ctx"),
            P("chan", "ctx"),
            P("chan", "ctx"),
            P("chan", None),
            P("chan"),
        ),
        check_vma=False,
    )
```

profile of v0, /device:TPU:1, one launch (start us, length us, event | category | flops | bytes accessed | tf_op | source)
XLA Modules:
  0.0 497.2 jit_solution(16550516221013616435)
XLA Ops:
  9.2 4.5 collective-permute-start
  16.0 41.6 %all-gather.2.cloned.1.call-done = f32[2048,256]{1,0:T(8,128)} async-done(((f32[512,256]{1,0:T(8,128)}), f32[2048,256]{1,0:T(8,128)}) %all-gather.2.cloned.1.call-update) | async-done | bytes 2097168 | tf_op jit(solution)/shard_map/all_gather | solution.py:171
  57.6 8.1 %multiply_reduce_fusion = (f32[512]{0:T(512)S(1)}, f32[512,256]{0,1:T(8,128)}, f32[512,256]{0,1:T(8,128)S(1)}, f32[512,256]{0,1:T(8,128)}) fusion(f32[512,256]{0,1:T(8,128)S(1)} %copy.214, f32[512,256]{0,1:T(8,128)S(1)} %copy.185, f32[512,6]{0,1:T(8,128)S(1)} %collective-permute-done, f32[512]{0:T(512)S(1)} %bitcast.367, f32[512]{0:T(512)S(1)} %bitcast.369, ...), kind=kOutput, calls=%fused_computation.166 | convolution fusion | flops 3224108544 | bytes 8941568 | tf_op jit(solution)/shard_map/dot_general | solution.py:169
  65.7 4.3 all-to-all-start.4
  71.5 5.3 %all-to-all-done.4 = f32[1,8,32,512]{3,2,0,1:T(8,128)S(1)} async-done(((f32[1,8,32,512]{3,2,0,1:T(8,128)}), f32[1,8,32,512]{3,2,0,1:T(8,128)S(1)}, u32[]{:S(2)}, u32[]{:S(2)}) %all-to-all-start.4) | async-done | bytes 524320 | tf_op jit(solution)/shard_map/all_to_all | solution.py:107
  76.7 6.5 %all-to-all-start = ((f32[2,8,32,512]{3,2,0,1:T(8,128)}), f32[2,8,32,512]{3,2,0,1:T(8,128)S(1)}, u32[]{:S(2)}, u32[]{:S(2)}) async-start(f32[2,8,32,512]{3,2,0,1:T(8,128)} %copy.188), calls=%async_computation | async-start | bytes 2097152 | tf_op jit(solution)/shard_map/all_to_all | solution.py:107
  89.1 6.0 %all-to-all-done = f32[2,8,32,512]{3,2,0,1:T(8,128)S(1)} async-done(((f32[2,8,32,512]{3,2,0,1:T(8,128)}), f32[2,8,32,512]{3,2,0,1:T(8,128)S(1)}, u32[]{:S(2)}, u32[]{:S(2)}) %all-to-all-start) | async-done | bytes 1048608 | tf_op jit(solution)/shard_map/all_to_all | solution.py:107
  95.1 7.3 %all-to-all-start.5 = ((f32[2,1,16,32,512]{4,3,1,0,2:T(8,128)}), f32[2,1,16,32,512]{4,3,1,0,2:T(8,128)S(1)}, u32[]{:S(2)}, u32[]{:S(2)}) async-start(f32[2,1,16,32,512]{4,3,1,0,2:T(8,128)} %copy.217), calls=%async_computation.5 | async-start | bytes 4194304 | tf_op jit(solution)/shard_map/all_to_all | solution.py:113
  108.6 4.4 copy.191
  113.0 12.5 %all-to-all-done.5 = f32[2,1,16,32,512]{4,3,1,0,2:T(8,128)S(1)} async-done(((f32[2,1,16,32,512]{4,3,1,0,2:T(8,128)}), f32[2,1,16,32,512]{4,3,1,0,2:T(8,128)S(1)}, u32[]{:S(2)}, u32[]{:S(2)}) %all-to-all-start.5) | async-done | bytes 2097184 | tf_op jit(solution)/shard_map/all_to_all | solution.py:113
  125.5 8.3 %all-to-all-start.1 = ((f32[2,2,16,32,512]{4,3,1,0,2:T(8,128)}), f32[2,2,16,32,512]{4,3,1,0,2:T(8,128)}, u32[]{:S(2)}, u32[]{:S(2)}) async-start(f32[2,2,16,32,512]{4,3,1,0,2:T(8,128)} %copy.191), calls=%async_computation.1 | async-start | bytes 8388608 | tf_op jit(solution)/shard_map/all_to_all | solution.py:113
  136.2 3.7 fusion.212
  139.9 3.8 fusion.48
  143.8 4.2 fusion.208
  148.0 6.0 %add_bitcast_fusion.2 = (f32[512,2,2,128]{3,2,1,0:T(2,128)S(1)}, f32[512,2,2,128]{3,2,1,0:T(2,128)S(1)}) fusion(f32[2,1,512,2,128]{4,0,3,2,1:T(2,128)S(1)} %fusion.48, f32[2,128]{1,0:T(2,128)S(1)} %get-tuple-element.83, f32[2,128]{1,0:T(2,128)S(1)} %get-tuple-element.84, f32[2,512,2,128]{3,0,2,1:T(2,128)S(1)} %fusion.208, f32[512,2,2,128]{3,2,1,0:T(2,128)} %copy-done.15), kind=kOutput, calls=%fused_computation.105 | convolution fusion | flops 8126520 | bytes 5244928 | tf_op jit(solution)/shard_map/...ac,ab->...bc/dot_general | solution.py:53
  159.8 19.6 %all-to-all-done.1 = f32[2,2,16,32,512]{4,3,1,0,2:T(8,128)} async-done(((f32[2,2,16,32,512]{4,3,1,0,2:T(8,128)}), f32[2,2,16,32,512]{4,3,1,0,2:T(8,128)}, u32[]{:S(2)}, u32[]{:S(2)}) %all-to-all-start.1) | async-done | bytes 4194336 | tf_op jit(solution)/shard_map/all_to_all | solution.py:113
  187.9 8.8 %fusion.221 = f32[2,2,512,2,128]{4,0,3,2,1:T(2,128)} fusion(f32[2,512,2,2,128]{4,3,2,1,0:T(2,128)S(1)} %copy.258), kind=kOutput, calls=%fused_computation.285 | convolution fusion | flops 12582968 | bytes 4194304 | tf_op jit(solution)/shard_map/...ac,ab->...bc/dot_general | solution.py:53
  196.7 8.7 %fusion.223 = f32[2,2,512,2,128]{4,0,3,2,1:T(2,128)} fusion(f32[2,512,2,2,128]{4,3,2,1,0:T(2,128)S(1)} %copy.258), kind=kOutput, calls=%fused_computation.287 | convolution fusion | flops 12582972 | bytes 4194304 | tf_op jit(solution)/shard_map/...ac,ab->...bc/dot_general | solution.py:53
  208.5 9.6 %convolution_subtract_fusion = f32[2,2,512,2,128]{4,0,3,2,1:T(2,128)S(1)} fusion(f32[2,2,512,2,128]{4,0,3,2,1:T(2,128)} %fusion.221, f32[2,512,2,2,128]{4,3,2,1,0:T(2,128)S(1)} %copy.259), kind=kOutput, calls=%fused_computation.43 | convolution fusion | flops 13107260 | bytes 6291456 | tf_op jit(solution)/shard_map/...ac,ab->...bc/dot_general | solution.py:53
  218.1 9.9 %subtract_bitcast_fusion.1 = (f32[2,512,2,2,128]{4,3,2,1,0:T(2,128)S(1)}, f32[2,512,2,2,128]{4,3,2,1,0:T(2,128)S(1)}) fusion(f32[2,2,512,2,128]{4,0,3,2,1:T(2,128)S(1)} %convolution_subtract_fusion, f32[2,128]{1,0:T(2,128)S(1)} %get-tuple-element.83, f32[2,128]{1,0:T(2,128)S(1)} %get-tuple-element.84, f32[2,2,512,2,128]{4,0,3,2,1:T(2,128)S(1)} %copy-done.12, ...), kind=kOutput, calls=%fused_computation.27 | convolution fusion | flops 16252984 | bytes 10487808 | tf_op jit(solution)/shard_map/...ac,ab->...bc/dot_general | solution.py:53
  243.6 4.9 fusion.81
  248.5 5.9 %fusion.79 = f32[2,512,2,128]{3,0,2,1:T(2,128)} fusion(f32[512,2,2,128]{3,0,2,1:T(8,128)S(1)} %get-tuple-element.66), kind=kOutput, calls=%fused_computation.127 | convolution fusion | flops 6291512 | bytes 2097152 | tf_op jit(solution)/shard_map/...ac,ab->...bc/dot_general | solution.py:53
  254.5 3.4 fusion.20
  257.9 3.4 fusion.21
  261.3 6.0 %fusion.50 = f32[1,512,2,2,128]{4,3,2,1,0:T(2,128)} fusion(f32[2,512,2,128]{3,0,2,1:T(2,128)S(1)} %fusion.81, f32[512,2,2,128]{3,0,2,1:T(8,128)S(1)} %get-tuple-element.65), kind=kOutput, calls=%fused_computation.80 | convolution fusion | flops 6553656 | bytes 3145728 | tf_op jit(solution)/shard_map/...ac,ab->...bc/dot_general | solution.py:53
  269.8 7.0 %fusion.49 = f32[1,512,2,2,128]{4,3,2,1,0:T(2,128)} fusion(f32[2,512,2,128]{3,0,2,1:T(2,128)} %fusion.79, f32[512,2,2,128]{3,0,2,1:T(8,128)} %copy-done.14), kind=kOutput, calls=%fused_computation.78 | convolution fusion | flops 6553656 | bytes 3145728 | tf_op jit(solution)/shard_map/...ac,ab->...bc/dot_general | solution.py:53
  276.8 4.0 copy.261
  280.8 3.5 maximum_bitcast_fusion.1
  284.3 7.9 %all-to-all-start.2 = ((f32[2,1,2,256,512]{4,2,0,1,3:T(2,128)}), f32[2,1,2,256,512]{4,2,0,1,3:T(2,128)}, u32[]{:S(2)}, u32[]{:S(2)}) async-start(f32[2,1,2,256,512]{4,2,0,1,3:T(2,128)} %maximum_bitcast_fusion.1), calls=%async_computation.2 | async-start | bytes 4194304 | tf_op jit(solution)/shard_map/all_to_all | solution.py:128
  292.2 3.8 fusion.24
  296.0 3.7 multiply_add_fusion
  299.7 8.1 %fusion.36 = f32[2,2,512,2,128]{4,0,3,2,1:T(2,128)S(1)} fusion(f32[2,512,2,2,128]{4,1,3,2,0:T(8,128)S(1)} %get-tuple-element.50), kind=kOutput, calls=%fused_computation.50 | convolution fusion | flops 12582968 | bytes 4194304 | tf_op jit(solution)/shard_map/...ac,ab->...bc/dot_general | solution.py:53
  307.8 9.8 %subtract_bitcast_fusion = f32[2,512,2,2,128]{4,3,2,1,0:T(2,128)} fusion(f32[2,2,512,2,128]{4,0,3,2,1:T(2,128)S(1)} %fusion.36, f32[2,512,2,2,128]{4,1,3,2,0:T(8,128)S(1)} %get-tuple-element.49), kind=kOutput, calls=%fused_computation.23 | convolution fusion | flops 13107256 | bytes 6291456 | tf_op jit(solution)/shard_map/...ac,ab->...bc/dot_general | solution.py:53
  317.6 6.1 %copy.264 = f32[2,512,2,2,128]{1,2,0,4,3:T(2,128)} copy(f32[2,512,2,2,128]{4,3,2,1,0:T(2,128)} %subtract_bitcast_fusion) | data formatting | bytes 4194304 | tf_op jit(solution)/shard_map/stack;reshape | solution.py:127
  323.7 8.0 %fusion.34 = f32[2,2,512,2,128]{4,0,3,2,1:T(2,128)S(1)} fusion(f32[2,512,2,2,128]{4,1,3,2,0:T(8,128)S(1)} %get-tuple-element.50), kind=kOutput, calls=%fused_computation.48 | convolution fusion | flops 12582968 | bytes 4194304 | tf_op jit(solution)/shard_map/...ac,ab->...bc/dot_general | solution.py:53
  331.8 9.9 %add_bitcast_fusion = f32[2,512,2,2,128]{4,3,2,1,0:T(2,128)} fusion(f32[2,2,512,2,128]{4,0,3,2,1:T(2,128)S(1)} %fusion.34, f32[2,512,2,2,128]{4,1,3,2,0:T(8,128)S(1)} %copy-done.11), kind=kOutput, calls=%fused_computation.22 | convolution fusion | flops 13107256 | bytes 6291456 | tf_op jit(solution)/shard_map/...ac,ab->...bc/dot_general | solution.py:53
  341.7 6.3 %copy.265 = f32[2,512,2,2,128]{1,2,0,4,3:T(2,128)} copy(f32[2,512,2,2,128]{4,3,2,1,0:T(2,128)} %add_bitcast_fusion) | data formatting | bytes 4194304 | tf_op jit(solution)/shard_map/stack;reshape | solution.py:127
  347.9 5.7 %maximum_bitcast_fusion = f32[2,2,2,256,512]{4,2,1,0,3:T(2,128)} fusion(f32[1,2,512,2,256]{2,3,1,0,4:T(2,128)} %bitcast.348, f32[1,2,512,2,256]{2,3,1,0,4:T(2,128)S(1)} %bitcast.345), kind=kLoop, calls=%fused_computation.1 | loop fusion | flops 1048576 | bytes 8388608 | tf_op jit(solution)/shard_map/transpose | solution.py:127
  353.6 4.6 all-to-all-start.6
  365.2 38.7 %all-to-all-done.6 = f32[2,2,2,256,512]{4,2,1,0,3:T(2,128)} async-done(((f32[2,2,2,256,512]{4,2,1,0,3:T(2,128)}), f32[2,2,2,256,512]{4,2,1,0,3:T(2,128)}, u32[]{:S(2)}, u32[]{:S(2)}) %all-to-all-start.6) | async-done | bytes 4194336 | tf_op jit(solution)/shard_map/all_to_all | solution.py:128
  403.9 7.3 %all-to-all-start.3 = ((f32[1,8,32,512]{3,2,0,1:T(8,128)}), f32[1,8,32,512]{3,2,0,1:T(8,128)S(1)}, u32[]{:S(2)}, u32[]{:S(2)}) async-start(f32[1,8,32,512]{3,2,0,1:T(8,128)} %copy.213), calls=%async_computation.3 | async-start | bytes 1048576 | tf_op jit(solution)/shard_map/all_to_all | solution.py:135
  411.2 4.6 copy.232
  423.4 4.5 copy.234
  428.0 3.6 squeeze.27
  438.1 4.2 all-to-all-start.7
  442.4 11.9 %all-to-all-done.7 = f32[2,8,32,512]{3,2,0,1:T(8,128)S(1)} async-done(((f32[2,8,32,512]{3,2,0,1:T(8,128)}), f32[2,8,32,512]{3,2,0,1:T(8,128)S(1)}, u32[]{:S(2)}, u32[]{:S(2)}) %all-to-all-start.7) | async-done | bytes 1048608 | tf_op jit(solution)/shard_map/all_to_all | solution.py:135
  457.5 22.6 %all-reduce = (f32[512,7]{0,1:T(8,128)S(1)}, f32[512]{0:T(512)S(1)}) all-reduce(f32[512,7]{0,1:T(8,128)S(1)} %stack.87, f32[512]{0:T(512)S(1)} %get-tuple-element.39), channel_id=1, replica_groups=mesh['ctx'=8,'chan'=4] {'ctx'}, use_global_device_ids=true, to_apply=%region_7.8 | all-reduce | flops 4096 | bytes 32768 | tf_op jit(solution)/shard_map/psum | solution.py:204
  480.7 5.1 %collective-permute-start.1 = (f32[512,6]{0,1:T(8,128)S(1)}, f32[512,6]{0,1:T(8,128)S(1)}, u32[]{:S(2)}, u32[]{:S(2)}) collective-permute-start(f32[512,6]{0,1:T(8,128)S(1)} %slice.185), channel_id=1, source_target_pairs={{4,0},{8,4},{12,8},{16,12},{20,16},{24,20},{28,24},{5,1},{9,5},{13... | collective-permute-start | bytes 36872 | tf_op jit(solution)/shard_map/ppermute | solution.py:13
  (112 shorter events, 84.2 us)
Async XLA Ops:
  7.2 50.5 %all-gather.2.cloned.1.call-start = ((), (), s32[]{:S(2)}) async-start(), calls=%async_computation.8 | async-start | bytes 2621440 | tf_op jit(solution)/shard_map/all_gather | solution.py:171
  9.1 56.6 %copy-start.4 = (f32[512,256]{0,1:T(8,128)}, f32[512,256]{0,1:T(8,128)S(1)}, u32[]{:S(2)}) copy-start(f32[512,256]{0,1:T(8,128)S(1)} %copy.185) | copy-start | bytes 1572868
  9.2 6.8 %collective-permute-start = (f32[512,6]{0,1:T(8,128)S(1)}, f32[512,6]{0,1:T(8,128)S(1)}, u32[]{:S(2)}, u32[]{:S(2)}) collective-permute-start(f32[512,6]{0,1:T(8,128)S(1)} %slice.161), channel_id=1, source_target_pairs={{0,4},{4,8},{8,12},{12,16},{16,20},{20,24},{24,28},{1,5},{5,9},{9,... | collective-permute-start | bytes 36872 | tf_op jit(solution)/shard_map/ppermute | solution.py:13
  57.6 12.4 %copy-start.16 = (f32[512,256]{1,0:T(8,128)S(1)}, f32[512,256]{1,0:T(8,128)}, u32[]{:S(2)}) copy-start(f32[512,256]{1,0:T(8,128)} %param.9) | copy-start | bytes 1572868
  65.7 4.7 copy-start.6
  65.7 11.0 %all-to-all-start.4 = ((f32[1,8,32,512]{3,2,0,1:T(8,128)}), f32[1,8,32,512]{3,2,0,1:T(8,128)S(1)}, u32[]{:S(2)}, u32[]{:S(2)}) async-start(f32[1,8,32,512]{3,2,0,1:T(8,128)} %bitcast.75), calls=%async_computation.4 | async-start | bytes 1048576 | tf_op jit(solution)/shard_map/all_to_all | solution.py:107
  76.7 18.4 %all-to-all-start = ((f32[2,8,32,512]{3,2,0,1:T(8,128)}), f32[2,8,32,512]{3,2,0,1:T(8,128)S(1)}, u32[]{:S(2)}, u32[]{:S(2)}) async-start(f32[2,8,32,512]{3,2,0,1:T(8,128)} %copy.188), calls=%async_computation | async-start | bytes 2097152 | tf_op jit(solution)/shard_map/all_to_all | solution.py:107
  95.1 30.4 %all-to-all-start.5 = ((f32[2,1,16,32,512]{4,3,1,0,2:T(8,128)}), f32[2,1,16,32,512]{4,3,1,0,2:T(8,128)S(1)}, u32[]{:S(2)}, u32[]{:S(2)}) async-start(f32[2,1,16,32,512]{4,3,1,0,2:T(8,128)} %copy.217), calls=%async_computation.5 | async-start | bytes 4194304 | tf_op jit(solution)/shard_map/all_to_all | solution.py:113
  125.5 53.9 %all-to-all-start.1 = ((f32[2,2,16,32,512]{4,3,1,0,2:T(8,128)}), f32[2,2,16,32,512]{4,3,1,0,2:T(8,128)}, u32[]{:S(2)}, u32[]{:S(2)}) async-start(f32[2,2,16,32,512]{4,3,1,0,2:T(8,128)} %copy.191), calls=%async_computation.1 | async-start | bytes 8388608 | tf_op jit(solution)/shard_map/all_to_all | solution.py:113
  136.2 7.6 %copy-start.15 = (f32[512,2,2,128]{3,2,1,0:T(2,128)}, f32[512,2,2,128]{3,2,1,0:T(2,128)S(1)}, u32[]{:S(2)}) copy-start(f32[512,2,2,128]{3,2,1,0:T(2,128)S(1)} %copy.263) | copy-start | bytes 3145732
  208.5 9.6 %copy-start.12 = (f32[2,2,512,2,128]{4,0,3,2,1:T(2,128)S(1)}, f32[2,2,512,2,128]{4,0,3,2,1:T(2,128)}, u32[]{:S(2)}) copy-start(f32[2,2,512,2,128]{4,0,3,2,1:T(2,128)} %fusion.223) | copy-start | bytes 6291460
  234.3 2.1 copy-start.8
  234.3 2.1 copy-start.9
  238.2 53.9 %copy-start.1 = (f32[1,512,2,2,128]{4,1,3,2,0:T(8,128)}, f32[1,512,2,2,128]{4,1,3,2,0:T(8,128)S(1)}, u32[]{:S(2)}) copy-start(f32[1,512,2,2,128]{4,1,3,2,0:T(8,128)S(1)} %get-tuple-element.46) | copy-start | bytes 3145732
  243.6 17.7 %copy-start.14 = (f32[512,2,2,128]{3,0,2,1:T(8,128)}, f32[512,2,2,128]{3,0,2,1:T(8,128)S(1)}, u32[]{:S(2)}) copy-start(f32[512,2,2,128]{3,0,2,1:T(8,128)S(1)} %get-tuple-element.65) | copy-start | bytes 3145732
  284.3 69.4 %all-to-all-start.2 = ((f32[2,1,2,256,512]{4,2,0,1,3:T(2,128)}), f32[2,1,2,256,512]{4,2,0,1,3:T(2,128)}, u32[]{:S(2)}, u32[]{:S(2)}) async-start(f32[2,1,2,256,512]{4,2,0,1,3:T(2,128)} %maximum_bitcast_fusion.1), calls=%async_computation.2 | async-start | bytes 4194304 | tf_op jit(solution)/shard_map/all_to_all | solution.py:128
  292.2 3.9 copy-start.2
  299.7 8.1 %copy-start.10 = (f32[2,512,2,2,128]{4,1,3,2,0:T(8,128)}, f32[2,512,2,2,128]{4,1,3,2,0:T(8,128)S(1)}, u32[]{:S(2)}) copy-start(f32[2,512,2,2,128]{4,1,3,2,0:T(8,128)S(1)} %get-tuple-element.49) | copy-start | bytes 6291460
  323.7 8.1 %copy-start.11 = (f32[2,512,2,2,128]{4,1,3,2,0:T(8,128)S(1)}, f32[2,512,2,2,128]{4,1,3,2,0:T(8,128)}, u32[]{:S(2)}) copy-start(f32[2,512,2,2,128]{4,1,3,2,0:T(8,128)} %copy-done.10) | copy-start | bytes 6291460
  341.7 6.3 %copy-start.3 = (f32[2,512,2,2,128]{1,2,0,4,3:T(2,128)S(1)}, f32[2,512,2,2,128]{1,2,0,4,3:T(2,128)}, u32[]{:S(2)}) copy-start(f32[2,512,2,2,128]{1,2,0,4,3:T(2,128)} %copy.264) | copy-start | bytes 6291460
  353.6 50.2 %all-to-all-start.6 = ((f32[2,2,2,256,512]{4,2,1,0,3:T(2,128)}), f32[2,2,2,256,512]{4,2,1,0,3:T(2,128)}, u32[]{:S(2)}, u32[]{:S(2)}) async-start(f32[2,2,2,256,512]{4,2,1,0,3:T(2,128)} %maximum_bitcast_fusion), calls=%async_computation.6 | async-start | bytes 8388608 | tf_op jit(solution)/shard_map/all_to_all | solution.py:128
  403.9 34.3 %all-to-all-start.3 = ((f32[1,8,32,512]{3,2,0,1:T(8,128)}), f32[1,8,32,512]{3,2,0,1:T(8,128)S(1)}, u32[]{:S(2)}, u32[]{:S(2)}) async-start(f32[1,8,32,512]{3,2,0,1:T(8,128)} %copy.213), calls=%async_computation.3 | async-start | bytes 1048576 | tf_op jit(solution)/shard_map/all_to_all | solution.py:135
  431.6 3.3 copy-start
  438.1 16.2 %all-to-all-start.7 = ((f32[2,8,32,512]{3,2,0,1:T(8,128)}), f32[2,8,32,512]{3,2,0,1:T(8,128)S(1)}, u32[]{:S(2)}, u32[]{:S(2)}) async-start(f32[2,8,32,512]{3,2,0,1:T(8,128)} %copy.235), calls=%async_computation.7 | async-start | bytes 2097152 | tf_op jit(solution)/shard_map/all_to_all | solution.py:135
  454.5 1.0 copy-start.5
  454.5 1.2 copy-start.7
  454.5 1.3 copy-start.13
  454.5 1.3 copy-start.17
  480.7 7.7 %collective-permute-start.1 = (f32[512,6]{0,1:T(8,128)S(1)}, f32[512,6]{0,1:T(8,128)S(1)}, u32[]{:S(2)}, u32[]{:S(2)}) collective-permute-start(f32[512,6]{0,1:T(8,128)S(1)} %slice.185), channel_id=1, source_target_pairs={{4,0},{8,4},{12,8},{16,12},{20,16},{24,20},{28,24},{5,1},{9,5},{13... | collective-permute-start | bytes 36872 | tf_op jit(solution)/shard_map/ppermute | solution.py:13
Sparse Core Ops, SparseCore 0:
  9.6 48.0 all-gather.1
where the time goes:
time: 506 us; the launch traced here: 497 us
  matrix products  174 us (34%)
  waiting for transfers between devices  136 us (27%)
  local copies, waits for them, and re-layouts  74.8 us (15%)
  starting transfers between devices  60.1 us (12%)
  blocking collectives  22.6 us (4%)
  between operations  15.2 us (3%)
  other arithmetic  14.5 us (3%)
    dot_general x16, matrix products, product_with(): return jnp.einsum('...ac,ab->...bc', operand, table, precision=HIGH)  114 us
    all_gather x1, waiting for transfers between devices, per_device(): lax.all_gather(cotangent, 'chan', axis=0, tiled=True)  41.6 us
    all_to_all x2, waiting for transfers between devices, signals(): lax.all_to_all(stacked, 'ctx', split_axis=3, concat_axis=2, tiled=True)  38.7 us
    dot_general x16, matrix products, product_with(): return jnp.einsum('...a,ab->...b', operand, table, precision=HIGH)  35.5 us
    all_to_all x2, waiting for transfers between devices, spectra(): lax.all_to_all(jnp.stack((real_part, imag_part)), 'ctx', split_axis=2, co...  32.1 us
    psum x1, blocking collectives, per_device(): skip_sum, kernel_sum = lax.psum((skip_part, kernel_part), 'ctx')  22.6 us
    another operation x4, local copies, waits for them, and re-layouts, signals(): stacked = jnp.moveaxis(jnp.stack((real_part, imag_part)), 2, 4)  18.9 us
    all_to_all x2, starting transfers between devices, spectra(): lax.all_to_all(jnp.stack((real_part, imag_part)), 'ctx', split_axis=2, co...  15.6 us
  transfers between devices with their start and end apart: 11, of which 7 were waited for; matrix products, arithmetic and copies ran while one was open for 29% of the time, Pallas kernels for 0%

commit v1 on v0

--- a/solution.py
+++ b/solution.py
@@ -5,6 +5,19 @@
 from jax.sharding import PartitionSpec as P
 
 HIGH = lax.Precision.HIGHEST
+
+
+def collect(x, axis, dim):
+    ways = lax.axis_size(axis)
+    up = [(d, (d + 1) % ways) for d in range(ways)]
+    down = [(d, (d - 1) % ways) for d in range(ways)]
+    earlier, later = ([x], [x])
+    for _ in range(ways // 2):
+        earlier.append(lax.ppermute(earlier[-1], axis, up))
+    for _ in range((ways - 1) // 2):
+        later.append(lax.ppermute(later[-1], axis, down))
+    line = jnp.concatenate([*earlier[::-1], *later[1:]], axis=dim)
+    return jnp.roll(line, (lax.axis_index(axis) - ways // 2) * x.shape[dim], axis=dim)
 
 
 def passed_along(block, axis, distance):
@@ -168,7 +181,7 @@
     long_conv = signals(conv_real[None], conv_imag[None])[0]
     grad_mix = jnp.dot(
         out_weight.T,
-        lax.all_gather(cotangent, "chan", axis=0, tiled=True),
+        collect(cotangent, "chan", 0),
         precision=HIGH,
         preferred_element_type=jnp.float32,
     )

time: 506 us -> 483 us (0.955)
  waiting for transfers between devices: 136 us -> 121 us
  between operations: 15.2 us -> 1.71 us
  starting transfers between devices: 60.1 us -> 67.2 us
    all_gather x1 -> x0, waiting for transfers between devices: 41.6 us -> none  [per_device(): lax.all_gather(cotangent, 'chan', axis=0, tiled=True)]
    ppermute x0 -> x3, waiting for transfers between devices: none -> 26.8 us  [the longest x2 17.3 us: collect(): earlier.append(lax.ppermute(earlier[-1], axis, up))]
    ppermute x0 -> x3, starting transfers between devices: none -> 5.44 us  [the longest x1 3.26 us: collect(): later.append(lax.ppermute(later[-1], axis, down))]
  transfers between devices with their start and end apart: 11 -> 13, of which waited for: 7 -> 9; matrix products, arithmetic and copies ran while one was open for 29% -> 30% of each run, Pallas kernels for 0% -> 0%
where the time goes in v1:
time: 483 us; the launch traced here: 474 us
  matrix products  171 us (35%)
  waiting for transfers between devices  121 us (25%)
  local copies, waits for them, and re-layouts  75.8 us (16%)
  starting transfers between devices  67.2 us (14%)
  blocking collectives  22.6 us (5%)
  other arithmetic  14.6 us (3%)
    dot_general x16, matrix products, product_with(): return jnp.einsum('...ac,ab->...bc', operand, table, precision=HIGH)  115 us
    all_to_all x2, waiting for transfers between devices, signals(): lax.all_to_all(stacked, 'ctx', split_axis=3, concat_axis=2, tiled=True)  38.7 us
    dot_general x16, matrix products, product_with(): return jnp.einsum('...a,ab->...b', operand, table, precision=HIGH)  35.6 us
    all_to_all x2, waiting for transfers between devices, spectra(): lax.all_to_all(jnp.stack((real_part, imag_part)), 'ctx', split_axis=2, co...  32.4 us
    psum x1, blocking collectives, per_device(): skip_sum, kernel_sum = lax.psum((skip_part, kernel_part), 'ctx')  22.6 us
    another operation x4, local copies, waits for them, and re-layouts, signals(): stacked = jnp.moveaxis(jnp.stack((real_part, imag_part)), 2, 4)  18.7 us
    ppermute x2, waiting for transfers between devices, collect(): earlier.append(lax.ppermute(earlier[-1], axis, up))  17.3 us
    all_to_all x2, starting transfers between devices, spectra(): lax.all_to_all(jnp.stack((real_part, imag_part)), 'ctx', split_axis=2, co...  15.8 us
  transfers between devices with their start and end apart: 13, of which 9 were waited for; matrix products, arithmetic and copies ran while one was open for 30% of the time, Pallas kernels for 0%

profile of v1, /device:TPU:1, one launch (start us, length us, event | category | flops | bytes accessed | tf_op | source)
XLA Modules:
  0.0 473.9 jit_solution(3074593121745470743)
XLA Ops:
  2.8 13.9 %collective-permute-done = f32[512,256]{1,0:T(8,128)S(1)} collective-permute-done((f32[512,256]{1,0:T(8,128)}, f32[512,256]{1,0:T(8,128)S(1)}, u32[]{:S(2)}, u32[]{:S(2)}) %collective-permute-start) | collective-permute-done | bytes 524320 | tf_op jit(solution)/shard_map/ppermute | solution.py:16
  21.2 4.8 %collective-permute-start.3 = (f32[512,6]{0,1:T(8,128)S(1)}, f32[512,6]{0,1:T(8,128)S(1)}, u32[]{:S(2)}, u32[]{:S(2)}) collective-permute-start(f32[512,6]{0,1:T(8,128)S(1)} %slice.161), channel_id=1, source_target_pairs={{0,4},{4,8},{8,12},{12,16},{16,20},{20,24},{24,28},{1,5},{5,9},{9,... | collective-permute-start | bytes 36872 | tf_op jit(solution)/shard_map/ppermute | solution.py:26
  30.9 9.4 %collective-permute-done.2 = f32[512,256]{1,0:T(8,128)S(1)} collective-permute-done((f32[512,256]{1,0:T(8,128)}, f32[512,256]{1,0:T(8,128)S(1)}, u32[]{:S(2)}, u32[]{:S(2)}) %collective-permute-start.2) | collective-permute-done | bytes 524320 | tf_op jit(solution)/shard_map/ppermute | solution.py:18
  42.6 5.0 %multiply_reduce_fusion = (f32[512]{0:T(512)S(1)}, f32[512,256]{0,1:T(8,128)}, f32[512,256]{0,1:T(8,128)S(1)}, f32[512,256]{0,1:T(8,128)}) fusion(f32[512,256]{0,1:T(8,128)S(1)} %copy.214, f32[512,256]{0,1:T(8,128)S(1)} %copy.185, f32[512,6]{0,1:T(8,128)S(1)} %collective-permute-done.3, f32[512]{0:T(512)S(1)} %bitcast.368, f32[512]{0:T(512)S(1)} %bitcast.370, ...), kind=kOutput, calls=%fused_computation.169 | convolution fusion | flops 3224108544 | bytes 8945668 | tf_op jit(solution)/shard_map/dot_general | solution.py:182
  47.6 5.6 %all-to-all-start.4 = ((f32[1,8,32,512]{3,2,0,1:T(8,128)}), f32[1,8,32,512]{3,2,0,1:T(8,128)S(1)}, u32[]{:S(2)}, u32[]{:S(2)}) async-start(f32[1,8,32,512]{3,2,0,1:T(8,128)} %bitcast.76), calls=%async_computation.4 | async-start | bytes 1048576 | tf_op jit(solution)/shard_map/all_to_all | solution.py:120
  54.6 5.3 %all-to-all-done.4 = f32[1,8,32,512]{3,2,0,1:T(8,128)S(1)} async-done(((f32[1,8,32,512]{3,2,0,1:T(8,128)}), f32[1,8,32,512]{3,2,0,1:T(8,128)S(1)}, u32[]{:S(2)}, u32[]{:S(2)}) %all-to-all-start.4) | async-done | bytes 524320 | tf_op jit(solution)/shard_map/all_to_all | solution.py:120
  59.9 6.5 %all-to-all-start = ((f32[2,8,32,512]{3,2,0,1:T(8,128)}), f32[2,8,32,512]{3,2,0,1:T(8,128)S(1)}, u32[]{:S(2)}, u32[]{:S(2)}) async-start(f32[2,8,32,512]{3,2,0,1:T(8,128)} %copy.188), calls=%async_computation | async-start | bytes 2097152 | tf_op jit(solution)/shard_map/all_to_all | solution.py:120
  72.3 6.0 %all-to-all-done = f32[2,8,32,512]{3,2,0,1:T(8,128)S(1)} async-done(((f32[2,8,32,512]{3,2,0,1:T(8,128)}), f32[2,8,32,512]{3,2,0,1:T(8,128)S(1)}, u32[]{:S(2)}, u32[]{:S(2)}) %all-to-all-start) | async-done | bytes 1048608 | tf_op jit(solution)/shard_map/all_to_all | solution.py:120
  78.3 7.6 %all-to-all-start.5 = ((f32[2,1,16,32,512]{4,3,1,0,2:T(8,128)}), f32[2,1,16,32,512]{4,3,1,0,2:T(8,128)S(1)}, u32[]{:S(2)}, u32[]{:S(2)}) async-start(f32[2,1,16,32,512]{4,3,1,0,2:T(8,128)} %copy.217), calls=%async_computation.5 | async-start | bytes 4194304 | tf_op jit(solution)/shard_map/all_to_all | solution.py:126
  92.1 4.4 copy.191
  96.5 12.5 %all-to-all-done.5 = f32[2,1,16,32,512]{4,3,1,0,2:T(8,128)S(1)} async-done(((f32[2,1,16,32,512]{4,3,1,0,2:T(8,128)}), f32[2,1,16,32,512]{4,3,1,0,2:T(8,128)S(1)}, u32[]{:S(2)}, u32[]{:S(2)}) %all-to-all-start.5) | async-done | bytes 2097184 | tf_op jit(solution)/shard_map/all_to_all | solution.py:126
  109.0 8.2 %all-to-all-start.1 = ((f32[2,2,16,32,512]{4,3,1,0,2:T(8,128)}), f32[2,2,16,32,512]{4,3,1,0,2:T(8,128)}, u32[]{:S(2)}, u32[]{:S(2)}) async-start(f32[2,2,16,32,512]{4,3,1,0,2:T(8,128)} %copy.191), calls=%async_computation.1 | async-start | bytes 8388608 | tf_op jit(solution)/shard_map/all_to_all | solution.py:126
  119.6 3.7 fusion.217
  123.3 3.8 fusion.50
  127.2 4.0 fusion.213
  131.1 6.0 %add_bitcast_fusion.2 = (f32[512,2,2,128]{3,2,1,0:T(2,128)S(1)}, f32[512,2,2,128]{3,2,1,0:T(2,128)S(1)}) fusion(f32[2,1,512,2,128]{4,0,3,2,1:T(2,128)S(1)} %fusion.50, f32[2,128]{1,0:T(2,128)S(1)} %get-tuple-element.83, f32[2,128]{1,0:T(2,128)S(1)} %get-tuple-element.84, f32[2,512,2,128]{3,0,2,1:T(2,128)S(1)} %fusion.213, f32[512,2,2,128]{3,2,1,0:T(2,128)} %copy-done.17), kind=kOutput, calls=%fused_computation.108 | convolution fusion | flops 8126520 | bytes 5244928 | tf_op jit(solution)/shard_map/...ac,ab->...bc/dot_general | solution.py:66
  142.9 19.9 %all-to-all-done.1 = f32[2,2,16,32,512]{4,3,1,0,2:T(8,128)} async-done(((f32[2,2,16,32,512]{4,3,1,0,2:T(8,128)}), f32[2,2,16,32,512]{4,3,1,0,2:T(8,128)}, u32[]{:S(2)}, u32[]{:S(2)}) %all-to-all-start.1) | async-done | bytes 4194336 | tf_op jit(solution)/shard_map/all_to_all | solution.py:126
  171.3 8.9 %fusion.226 = f32[2,2,512,2,128]{4,0,3,2,1:T(2,128)} fusion(f32[2,512,2,2,128]{4,3,2,1,0:T(2,128)S(1)} %copy.258), kind=kOutput, calls=%fused_computation.296 | convolution fusion | flops 12582968 | bytes 4194304 | tf_op jit(solution)/shard_map/...ac,ab->...bc/dot_general | solution.py:66
  180.2 8.7 %fusion.228 = f32[2,2,512,2,128]{4,0,3,2,1:T(2,128)} fusion(f32[2,512,2,2,128]{4,3,2,1,0:T(2,128)S(1)} %copy.258), kind=kOutput, calls=%fused_computation.298 | convolution fusion | flops 12582972 | bytes 4194304 | tf_op jit(solution)/shard_map/...ac,ab->...bc/dot_general | solution.py:66
  192.0 9.8 %convolution_subtract_fusion = f32[2,2,512,2,128]{4,0,3,2,1:T(2,128)S(1)} fusion(f32[2,2,512,2,128]{4,0,3,2,1:T(2,128)} %fusion.226, f32[2,512,2,2,128]{4,3,2,1,0:T(2,128)S(1)} %copy.259), kind=kOutput, calls=%fused_computation.45 | convolution fusion | flops 13107260 | bytes 6291456 | tf_op jit(solution)/shard_map/...ac,ab->...bc/dot_general | solution.py:66
  201.9 9.6 %subtract_bitcast_fusion.1 = (f32[2,512,2,2,128]{4,3,2,1,0:T(2,128)S(1)}, f32[2,512,2,2,128]{4,3,2,1,0:T(2,128)S(1)}) fusion(f32[2,2,512,2,128]{4,0,3,2,1:T(2,128)S(1)} %convolution_subtract_fusion, f32[2,128]{1,0:T(2,128)S(1)} %get-tuple-element.83, f32[2,128]{1,0:T(2,128)S(1)} %get-tuple-element.84, f32[2,2,512,2,128]{4,0,3,2,1:T(2,128)S(1)} %copy-done.13, ...), kind=kOutput, calls=%fused_computation.27 | convolution fusion | flops 16252984 | bytes 10487808 | tf_op jit(solution)/shard_map/...ac,ab->...bc/dot_general | solution.py:66
  227.2 4.9 %fusion.86 = f32[2,512,2,128]{3,0,2,1:T(2,128)S(1)} fusion(f32[512,2,2,128]{3,0,2,1:T(8,128)S(1)} %get-tuple-element.66), kind=kOutput, calls=%fused_computation.132 | convolution fusion | flops 6291512 | bytes 2097152 | tf_op jit(solution)/shard_map/...ac,ab->...bc/dot_general | solution.py:66
  232.1 6.1 %fusion.84 = f32[2,512,2,128]{3,0,2,1:T(2,128)} fusion(f32[512,2,2,128]{3,0,2,1:T(8,128)S(1)} %get-tuple-element.66), kind=kOutput, calls=%fused_computation.130 | convolution fusion | flops 6291512 | bytes 2097152 | tf_op jit(solution)/shard_map/...ac,ab->...bc/dot_general | solution.py:66
  238.2 3.4 fusion.22
  245.1 5.9 %fusion.52 = f32[1,512,2,2,128]{4,3,2,1,0:T(2,128)} fusion(f32[2,512,2,128]{3,0,2,1:T(2,128)S(1)} %fusion.86, f32[512,2,2,128]{3,0,2,1:T(8,128)S(1)} %get-tuple-element.65), kind=kOutput, calls=%fused_computation.82 | convolution fusion | flops 6553656 | bytes 3145728 | tf_op jit(solution)/shard_map/...ac,ab->...bc/dot_general | solution.py:66
  253.5 7.0 %fusion.51 = f32[1,512,2,2,128]{4,3,2,1,0:T(2,128)} fusion(f32[2,512,2,128]{3,0,2,1:T(2,128)} %fusion.84, f32[512,2,2,128]{3,0,2,1:T(8,128)} %copy-done.16), kind=kOutput, calls=%fused_computation.80 | convolution fusion | flops 6553656 | bytes 3145728 | tf_op jit(solution)/shard_map/...ac,ab->...bc/dot_general | solution.py:66
  260.6 3.8 copy.261
  264.3 3.5 maximum_bitcast_fusion.1
  267.9 7.9 %all-to-all-start.2 = ((f32[2,1,2,256,512]{4,2,0,1,3:T(2,128)}), f32[2,1,2,256,512]{4,2,0,1,3:T(2,128)}, u32[]{:S(2)}, u32[]{:S(2)}) async-start(f32[2,1,2,256,512]{4,2,0,1,3:T(2,128)} %maximum_bitcast_fusion.1), calls=%async_computation.2 | async-start | bytes 4194304 | tf_op jit(solution)/shard_map/all_to_all | solution.py:141
  275.7 3.8 fusion.26
  279.6 3.7 multiply_add_fusion
  283.3 8.1 %fusion.38 = f32[2,2,512,2,128]{4,0,3,2,1:T(2,128)S(1)} fusion(f32[2,512,2,2,128]{4,1,3,2,0:T(8,128)S(1)} %get-tuple-element.50), kind=kOutput, calls=%fused_computation.52 | convolution fusion | flops 12582968 | bytes 4194304 | tf_op jit(solution)/shard_map/...ac,ab->...bc/dot_general | solution.py:66
  291.4 9.9 %subtract_bitcast_fusion = f32[2,512,2,2,128]{4,3,2,1,0:T(2,128)} fusion(f32[2,2,512,2,128]{4,0,3,2,1:T(2,128)S(1)} %fusion.38, f32[2,512,2,2,128]{4,1,3,2,0:T(8,128)S(1)} %get-tuple-element.49), kind=kOutput, calls=%fused_computation.23 | convolution fusion | flops 13107256 | bytes 6291456 | tf_op jit(solution)/shard_map/...ac,ab->...bc/dot_general | solution.py:66
  301.3 6.1 %copy.264 = f32[2,512,2,2,128]{1,2,0,4,3:T(2,128)} copy(f32[2,512,2,2,128]{4,3,2,1,0:T(2,128)} %subtract_bitcast_fusion) | data formatting | bytes 4194304 | tf_op jit(solution)/shard_map/stack;reshape | solution.py:140
  307.4 8.0 %fusion.36 = f32[2,2,512,2,128]{4,0,3,2,1:T(2,128)S(1)} fusion(f32[2,512,2,2,128]{4,1,3,2,0:T(8,128)S(1)} %get-tuple-element.50), kind=kOutput, calls=%fused_computation.50 | convolution fusion | flops 12582968 | bytes 4194304 | tf_op jit(solution)/shard_map/...ac,ab->...bc/dot_general | solution.py:66
  315.4 10.1 %add_bitcast_fusion = f32[2,512,2,2,128]{4,3,2,1,0:T(2,128)} fusion(f32[2,2,512,2,128]{4,0,3,2,1:T(2,128)S(1)} %fusion.36, f32[2,512,2,2,128]{4,1,3,2,0:T(8,128)S(1)} %copy-done.12), kind=kOutput, calls=%fused_computation.22 | convolution fusion | flops 13107256 | bytes 6291456 | tf_op jit(solution)/shard_map/...ac,ab->...bc/dot_general | solution.py:66
  325.5 6.3 %copy.265 = f32[2,512,2,2,128]{1,2,0,4,3:T(2,128)} copy(f32[2,512,2,2,128]{4,3,2,1,0:T(2,128)} %add_bitcast_fusion) | data formatting | bytes 4194304 | tf_op jit(solution)/shard_map/stack;reshape | solution.py:140
  331.8 5.7 %maximum_bitcast_fusion = f32[2,2,2,256,512]{4,2,1,0,3:T(2,128)} fusion(f32[1,2,512,2,256]{2,3,1,0,4:T(2,128)} %bitcast.349, f32[1,2,512,2,256]{2,3,1,0,4:T(2,128)S(1)} %bitcast.346), kind=kLoop, calls=%fused_computation.1 | loop fusion | flops 1048576 | bytes 8388608 | tf_op jit(solution)/shard_map/transpose | solution.py:140
  337.5 4.6 all-to-all-start.6
  349.0 38.7 %all-to-all-done.6 = f32[2,2,2,256,512]{4,2,1,0,3:T(2,128)} async-done(((f32[2,2,2,256,512]{4,2,1,0,3:T(2,128)}), f32[2,2,2,256,512]{4,2,1,0,3:T(2,128)}, u32[]{:S(2)}, u32[]{:S(2)}) %all-to-all-start.6) | async-done | bytes 4194336 | tf_op jit(solution)/shard_map/all_to_all | solution.py:141
  387.7 7.2 %all-to-all-start.3 = ((f32[1,8,32,512]{3,2,0,1:T(8,128)}), f32[1,8,32,512]{3,2,0,1:T(8,128)S(1)}, u32[]{:S(2)}, u32[]{:S(2)}) async-start(f32[1,8,32,512]{3,2,0,1:T(8,128)} %copy.213), calls=%async_computation.3 | async-start | bytes 1048576 | tf_op jit(solution)/shard_map/all_to_all | solution.py:148
  394.9 4.6 copy.232
  407.2 4.5 copy.234
  411.7 3.6 squeeze.27
  421.9 4.2 all-to-all-start.7
  426.2 11.9 %all-to-all-done.7 = f32[2,8,32,512]{3,2,0,1:T(8,128)S(1)} async-done(((f32[2,8,32,512]{3,2,0,1:T(8,128)}), f32[2,8,32,512]{3,2,0,1:T(8,128)S(1)}, u32[]{:S(2)}, u32[]{:S(2)}) %all-to-all-start.7) | async-done | bytes 1048608 | tf_op jit(solution)/shard_map/all_to_all | solution.py:148
  441.3 22.6 %all-reduce = (f32[512,7]{0,1:T(8,128)S(1)}, f32[512]{0:T(512)S(1)}) all-reduce(f32[512,7]{0,1:T(8,128)S(1)} %stack.87, f32[512]{0:T(512)S(1)} %get-tuple-element.39), channel_id=1, replica_groups=mesh['ctx'=8,'chan'=4] {'ctx'}, use_global_device_ids=true, to_apply=%region_7.8 | all-reduce | flops 4096 | bytes 32768 | tf_op jit(solution)/shard_map/psum | solution.py:217
  464.5 5.1 %collective-permute-start.4 = (f32[512,6]{0,1:T(8,128)S(1)}, f32[512,6]{0,1:T(8,128)S(1)}, u32[]{:S(2)}, u32[]{:S(2)}) collective-permute-start(f32[512,6]{0,1:T(8,128)S(1)} %slice.185), channel_id=1, source_target_pairs={{4,0},{8,4},{12,8},{16,12},{20,16},{24,20},{28,24},{5,1},{9,5},{13... | collective-permute-start | bytes 36872 | tf_op jit(solution)/shard_map/ppermute | solution.py:26
  (129 shorter events, 97.0 us)
Async XLA Ops:
  0.6 30.2 %copy-start.14 = (f32[512,256]{1,0:T(8,128)S(1)}, f32[512,256]{1,0:T(8,128)}, u32[]{:S(2)}) copy-start(f32[512,256]{1,0:T(8,128)} %param.13) | copy-start | bytes 1572868
  0.6 26.7 %copy-start.19 = (f32[512,7]{0,1:T(8,128)S(1)}, f32[512,7]{0,1:T(8,128)}, u32[]{:S(2)}) copy-start(f32[512,7]{0,1:T(8,128)} %param.10) | copy-start | bytes 43012
  0.7 16.1 %collective-permute-start = (f32[512,256]{1,0:T(8,128)}, f32[512,256]{1,0:T(8,128)S(1)}, u32[]{:S(2)}, u32[]{:S(2)}) collective-permute-start(f32[512,256]{1,0:T(8,128)} %param.13), channel_id=1, source_target_pairs={{0,1},{1,2},{2,3},{3,0},{4,5},{5,6},{6,7},{7,4},{8,9},{9,10},{10,1... | collective-permute-start | bytes 1572872 | tf_op jit(solution)/shard_map/ppermute | solution.py:16
  16.7 14.1 %collective-permute-start.1 = (f32[512,256]{1,0:T(8,128)S(1)}, f32[512,256]{1,0:T(8,128)S(1)}, u32[]{:S(2)}, u32[]{:S(2)}) collective-permute-start(f32[512,256]{1,0:T(8,128)S(1)} %collective-permute-done), channel_id=1, source_target_pairs={{0,1},{1,2},{2,3},{3,0},{4,5},{5,6},{6,7},{7,4},{8,9},{9,10},{10,1... | collective-permute-start | bytes 1572872 | tf_op jit(solution)/shard_map/ppermute | solution.py:16
  16.7 23.6 %collective-permute-start.2 = (f32[512,256]{1,0:T(8,128)}, f32[512,256]{1,0:T(8,128)S(1)}, u32[]{:S(2)}, u32[]{:S(2)}) collective-permute-start(f32[512,256]{1,0:T(8,128)} %param.13), channel_id=1, source_target_pairs={{0,3},{1,0},{2,1},{3,2},{4,7},{5,4},{6,5},{7,6},{8,11},{9,8},{10,9... | collective-permute-start | bytes 1572872 | tf_op jit(solution)/shard_map/ppermute | solution.py:18
  21.2 19.4 %copy-start.4 = (f32[512,256]{0,1:T(8,128)}, f32[512,256]{0,1:T(8,128)S(1)}, u32[]{:S(2)}) copy-start(f32[512,256]{0,1:T(8,128)S(1)} %copy.185) | copy-start | bytes 1572868
  21.2 19.3 %collective-permute-start.3 = (f32[512,6]{0,1:T(8,128)S(1)}, f32[512,6]{0,1:T(8,128)S(1)}, u32[]{:S(2)}, u32[]{:S(2)}) collective-permute-start(f32[512,6]{0,1:T(8,128)S(1)} %slice.161), channel_id=1, source_target_pairs={{0,4},{4,8},{8,12},{12,16},{16,20},{20,24},{24,28},{1,5},{5,9},{9,... | collective-permute-start | bytes 36872 | tf_op jit(solution)/shard_map/ppermute | solution.py:26
  40.4 2.2 copy-start.8
  42.6 10.6 %copy-start.18 = (f32[512,256]{1,0:T(8,128)S(1)}, f32[512,256]{1,0:T(8,128)}, u32[]{:S(2)}) copy-start(f32[512,256]{1,0:T(8,128)} %param.9) | copy-start | bytes 1572868
  47.6 6.0 %copy-start.6 = (f32[512,256]{0,1:T(8,128)}, f32[512,256]{0,1:T(8,128)S(1)}, u32[]{:S(2)}) copy-start(f32[512,256]{0,1:T(8,128)S(1)} %get-tuple-element.41) | copy-start | bytes 1572868
  47.6 12.3 %all-to-all-start.4 = ((f32[1,8,32,512]{3,2,0,1:T(8,128)}), f32[1,8,32,512]{3,2,0,1:T(8,128)S(1)}, u32[]{:S(2)}, u32[]{:S(2)}) async-start(f32[1,8,32,512]{3,2,0,1:T(8,128)} %bitcast.76), calls=%async_computation.4 | async-start | bytes 1048576 | tf_op jit(solution)/shard_map/all_to_all | solution.py:120
  59.9 18.4 %all-to-all-start = ((f32[2,8,32,512]{3,2,0,1:T(8,128)}), f32[2,8,32,512]{3,2,0,1:T(8,128)S(1)}, u32[]{:S(2)}, u32[]{:S(2)}) async-start(f32[2,8,32,512]{3,2,0,1:T(8,128)} %copy.188), calls=%async_computation | async-start | bytes 2097152 | tf_op jit(solution)/shard_map/all_to_all | solution.py:120
  78.3 30.7 %all-to-all-start.5 = ((f32[2,1,16,32,512]{4,3,1,0,2:T(8,128)}), f32[2,1,16,32,512]{4,3,1,0,2:T(8,128)S(1)}, u32[]{:S(2)}, u32[]{:S(2)}) async-start(f32[2,1,16,32,512]{4,3,1,0,2:T(8,128)} %copy.217), calls=%async_computation.5 | async-start | bytes 4194304 | tf_op jit(solution)/shard_map/all_to_all | solution.py:126
  109.0 53.8 %all-to-all-start.1 = ((f32[2,2,16,32,512]{4,3,1,0,2:T(8,128)}), f32[2,2,16,32,512]{4,3,1,0,2:T(8,128)}, u32[]{:S(2)}, u32[]{:S(2)}) async-start(f32[2,2,16,32,512]{4,3,1,0,2:T(8,128)} %copy.191), calls=%async_computation.1 | async-start | bytes 8388608 | tf_op jit(solution)/shard_map/all_to_all | solution.py:126
  119.6 7.6 %copy-start.17 = (f32[512,2,2,128]{3,2,1,0:T(2,128)}, f32[512,2,2,128]{3,2,1,0:T(2,128)S(1)}, u32[]{:S(2)}) copy-start(f32[512,2,2,128]{3,2,1,0:T(2,128)S(1)} %copy.263) | copy-start | bytes 3145732
  192.0 9.9 %copy-start.13 = (f32[2,2,512,2,128]{4,0,3,2,1:T(2,128)S(1)}, f32[2,2,512,2,128]{4,0,3,2,1:T(2,128)}, u32[]{:S(2)}) copy-start(f32[2,2,512,2,128]{4,0,3,2,1:T(2,128)} %fusion.228) | copy-start | bytes 6291460
  217.9 2.1 copy-start.9
  217.9 2.1 copy-start.10
  221.8 53.9 %copy-start.1 = (f32[1,512,2,2,128]{4,1,3,2,0:T(8,128)}, f32[1,512,2,2,128]{4,1,3,2,0:T(8,128)S(1)}, u32[]{:S(2)}) copy-start(f32[1,512,2,2,128]{4,1,3,2,0:T(8,128)S(1)} %get-tuple-element.46) | copy-start | bytes 3145732
  227.2 17.9 %copy-start.16 = (f32[512,2,2,128]{3,0,2,1:T(8,128)}, f32[512,2,2,128]{3,0,2,1:T(8,128)S(1)}, u32[]{:S(2)}) copy-start(f32[512,2,2,128]{3,0,2,1:T(8,128)S(1)} %get-tuple-element.65) | copy-start | bytes 3145732
  267.9 69.6 %all-to-all-start.2 = ((f32[2,1,2,256,512]{4,2,0,1,3:T(2,128)}), f32[2,1,2,256,512]{4,2,0,1,3:T(2,128)}, u32[]{:S(2)}, u32[]{:S(2)}) async-start(f32[2,1,2,256,512]{4,2,0,1,3:T(2,128)} %maximum_bitcast_fusion.1), calls=%async_computation.2 | async-start | bytes 4194304 | tf_op jit(solution)/shard_map/all_to_all | solution.py:141
  275.7 3.9 copy-start.2
  283.3 8.1 %copy-start.11 = (f32[2,512,2,2,128]{4,1,3,2,0:T(8,128)}, f32[2,512,2,2,128]{4,1,3,2,0:T(8,128)S(1)}, u32[]{:S(2)}) copy-start(f32[2,512,2,2,128]{4,1,3,2,0:T(8,128)S(1)} %get-tuple-element.49) | copy-start | bytes 6291460
  307.4 8.1 %copy-start.12 = (f32[2,512,2,2,128]{4,1,3,2,0:T(8,128)S(1)}, f32[2,512,2,2,128]{4,1,3,2,0:T(8,128)}, u32[]{:S(2)}) copy-start(f32[2,512,2,2,128]{4,1,3,2,0:T(8,128)} %copy-done.11) | copy-start | bytes 6291460
  325.5 6.3 %copy-start.3 = (f32[2,512,2,2,128]{1,2,0,4,3:T(2,128)S(1)}, f32[2,512,2,2,128]{1,2,0,4,3:T(2,128)}, u32[]{:S(2)}) copy-start(f32[2,512,2,2,128]{1,2,0,4,3:T(2,128)} %copy.264) | copy-start | bytes 6291460
  337.5 50.2 %all-to-all-start.6 = ((f32[2,2,2,256,512]{4,2,1,0,3:T(2,128)}), f32[2,2,2,256,512]{4,2,1,0,3:T(2,128)}, u32[]{:S(2)}, u32[]{:S(2)}) async-start(f32[2,2,2,256,512]{4,2,1,0,3:T(2,128)} %maximum_bitcast_fusion), calls=%async_computation.6 | async-start | bytes 8388608 | tf_op jit(solution)/shard_map/all_to_all | solution.py:141
  387.7 34.2 %all-to-all-start.3 = ((f32[1,8,32,512]{3,2,0,1:T(8,128)}), f32[1,8,32,512]{3,2,0,1:T(8,128)S(1)}, u32[]{:S(2)}, u32[]{:S(2)}) async-start(f32[1,8,32,512]{3,2,0,1:T(8,128)} %copy.213), calls=%async_computation.3 | async-start | bytes 1048576 | tf_op jit(solution)/shard_map/all_to_all | solution.py:148
  415.4 3.3 copy-start
  421.9 16.2 %all-to-all-start.7 = ((f32[2,8,32,512]{3,2,0,1:T(8,128)}), f32[2,8,32,512]{3,2,0,1:T(8,128)S(1)}, u32[]{:S(2)}, u32[]{:S(2)}) async-start(f32[2,8,32,512]{3,2,0,1:T(8,128)} %copy.235), calls=%async_computation.7 | async-start | bytes 2097152 | tf_op jit(solution)/shard_map/all_to_all | solution.py:148
  438.3 1.0 copy-start.5
  438.3 1.2 copy-start.7
  438.3 1.3 copy-start.15
  438.3 1.3 copy-start.20
  464.5 7.7 %collective-permute-start.4 = (f32[512,6]{0,1:T(8,128)S(1)}, f32[512,6]{0,1:T(8,128)S(1)}, u32[]{:S(2)}, u32[]{:S(2)}) collective-permute-start(f32[512,6]{0,1:T(8,128)S(1)} %slice.185), channel_id=1, source_target_pairs={{4,0},{8,4},{12,8},{16,12},{20,16},{24,20},{28,24},{5,1},{9,5},{13... | collective-permute-start | bytes 36872 | tf_op jit(solution)/shard_map/ppermute | solution.py:26
